TPU v7x, 256 devices: a whole 4x4x8 slice. The times are simulated.
256 devices in a mesh: region: 32 (over x, z), order: 8 (over y, core).
Axes of the slice: x: 4, y: 4, z: 8, core: 2. Of those that a mesh axis runs over, the one named last changes fastest.
Arguments:
- runoff: float32 [240, 32, 8192], P(None, None, ('region', 'order')), may hold values from 0.01 to 2
- send_rows: int32 [32, 8, 128], P('region', 'order'), may hold values from 0 to 31
- remap_index: int32 [32768, 4], P(('region', 'order')), may hold values from 0 to 127
- remap_weight: float32 [32768, 4], P(('region', 'order')), may hold values from 0.05 to 1
- class_id: int32 [32768, 1], P(('region', 'order')), may hold values from 0 to 7; in each aligned block of 128 rows (0 to 127, 128 to 255, ...) at most 32 rows name the same one
- kernel_shape: float32 [8, 240], replicated, may hold values from 0.5 to 2
- kernel_rate: float32 [8], replicated, may hold values from 0.01 to 0.3
- outlets: int32 [32, 8, 32], P('region', 'order'), may hold values from 0 to 127, as said below
- incidence: int32 [32, 8, 32, 128], P('region', 'order'), may hold values from 0 to 1, as said below
Outputs:
- outflow: bfloat16 [240, 32, 32768], P(None, None, ('region', 'order'))
Inputs may be any that keep to these rules, and one draw needn't show every extreme that they name: `send_rows`: row of the sending device's own grid rows. `class_id`: no class is named by more than 32 reaches of one device; on some device a class has exactly 32. `outlets`: the 32 outlet numbers of one device are distinct. `incidence`: each row has exactly one 1; no column of one device has more than one 1.
All inputs are finite; a program needn't handle non-finite values.
Results may differ from a plain program's by a relative error of at most 0.0038.
Values may be sent and summed in bfloat16 or wider, within the bound.
A program may use at most 128 MiB of HBM per device.

v0:
```python
import functools

import jax
import jax.numpy as jnp
from jax import lax
from jax.experimental import pallas as pl
from jax.experimental.pallas import tpu as pltpu
from jax.sharding import PartitionSpec as P

MESH = pl.DeviceIdType.MESH
BF = jnp.bfloat16
F32 = jnp.float32
LANES = 256
MG = 4


def mm(a, b):
    return jnp.dot(a, b, preferred_element_type=F32)


def mm_nt(a, b):
    return lax.dot_general(a, b, (((1,), (1,)), ((), ())), preferred_element_type=F32)


def iota(shape, dim):
    return lax.broadcasted_iota(jnp.int32, shape, dim)


def onehot(hits):
    return jnp.where(hits, 1.0, 0.0)


def kernel(
    sizes,
    x_ref,
    send_rows_ref,
    idx_ref,
    w_ref,
    cls_ref,
    shape_ref,
    rate_ref,
    outlets_ref,
    inc_ref,
    out_ref,
    xb,
    send,
    recv,
    inbox,
    outbox,
    lat,
    base_out,
    out32,
    sel,
    w_hi,
    w_lo,
    out_sel,
    perm,
    scat,
    mask_o,
    mask_c,
    toep,
    toep_t,
    ssem,
    rsem,
    cssem,
    crsem,
):
    hours, members, regions, orders, reaches, classes, panel = sizes
    groups = members // MG
    slots = send.shape[2] * regions
    r = lax.axis_index("region")
    o = lax.axis_index("order")
    nxt = lax.rem(o + 1, orders)
    prv = lax.rem(o + orders - 1, orders)

    barrier = pltpu.get_barrier_semaphore()

    def greet(d, c):
        peer = lax.rem(r + d, regions)
        pl.semaphore_signal(barrier, inc=1, device_id=(peer, o), device_id_type=MESH)
        return c

    lax.fori_loop(1, regions, greet, 0)
    pl.semaphore_signal(barrier, inc=1, device_id=(r, nxt), device_id_type=MESH)
    pl.semaphore_signal(barrier, inc=1, device_id=(r, prv), device_id_type=MESH)

    n0 = iota((slots, 128), 0)
    c1 = iota((slots, 128), 1)
    spread = onehot(c1 == (n0 >> 4) * 4 + (n0 & 3)).astype(BF)
    row_hit = onehot(send_rows_ref[...] == (iota((128, 128), 0) & 31)).astype(BF)
    picked = mm_nt(spread, row_hit)
    sel[...] = jnp.where(((n0 >> 2) & 3) == (c1 >> 5), picked, 0.0).astype(BF)
    xb[:, 128:LANES] = jnp.zeros((xb.shape[0], LANES - 128), BF)

    pl.semaphore_wait(barrier, regions + 1)

    def dispatch(g, c):
        rows = MG * 32
        start = pl.multiple_of(g * rows, rows)
        xb[:, 0:hours] = x_ref[pl.ds(start, rows), :].astype(BF)
        send[g] = mm(sel[...], xb[...]).astype(BF).reshape(send.shape[1:])
        pltpu.make_async_copy(send.at[g, r], recv.at[g, r], rsem.at[g]).start()

        def push(d, c):
            peer = lax.rem(r + d, regions)
            pltpu.make_async_remote_copy(
                src_ref=send.at[g, peer],
                dst_ref=recv.at[g, r],
                send_sem=ssem.at[g],
                recv_sem=rsem.at[g],
                device_id=(peer, o),
                device_id_type=MESH,
            ).start()
            return c

        return lax.fori_loop(1, regions, push, c)

    lax.fori_loop(0, groups, dispatch, 0)

    diag = iota((classes, classes), 0) == iota((classes, classes), 1)
    rate = jnp.sum(
        jnp.where(diag, jnp.broadcast_to(rate_ref[...], (classes, classes)), 0.0),
        axis=1,
        keepdims=True,
    )
    lag = iota((classes, hours), 1).astype(F32)
    unit = rate * shape_ref[...] * jnp.exp(-rate * lag)
    base_out[0:classes, 128:LANES] = jnp.zeros((classes, LANES - 128), F32)
    base_out[0:classes, 0:hours] = unit.astype(BF).astype(F32)
    later = iota((LANES, LANES), 1) >= iota((LANES, LANES), 0)

    def table(k, c):
        row = jnp.broadcast_to(base_out[pl.ds(k, 1), :], (LANES, LANES))
        turned = pltpu.roll(row, 0, 1, stride=1, stride_axis=0)
        turned = jnp.where(later, turned, 0.0)
        at = pl.multiple_of(k * LANES, LANES)
        toep_t[pl.ds(at, LANES), :] = turned.astype(BF)
        toep[:, pl.ds(at, LANES)] = turned.T.astype(BF)
        return c

    lax.fori_loop(0, classes, table, 0)

    pos = (n0 >> 4) * 4 + (n0 & 3)
    weights_t = jnp.zeros((slots, 128), F32)
    for j in range(4):
        weights_t = weights_t + jnp.where(idx_ref[j : j + 1, :] == pos, w_ref[j : j + 1, :], 0.0)
    weights = weights_t.T
    high = weights.astype(BF)
    low = (weights - high.astype(F32)).astype(BF)
    member_of = (iota((reaches, slots), 1) >> 2) & 3
    for m in range(MG):
        here = onehot(member_of == m).astype(BF)
        w_hi[m * 128 : (m + 1) * 128, :] = high * here
        w_lo[m * 128 : (m + 1) * 128, :] = low * here

    i0 = iota((128, 128), 0)
    i1 = iota((128, 128), 1)
    copies = onehot((iota((128, panel), 0) & 31) == iota((128, panel), 1)).astype(BF)
    at_outlet = onehot(outlets_ref[...] == iota((reaches, panel), 0)).astype(BF)
    outlet_of = mm_nt(copies, at_outlet)
    link_of = mm(copies, inc_ref[...].astype(F32).astype(BF))
    link_t = link_of.T
    for m in range(MG):
        out_sel[:, m * 128 : (m + 1) * 128] = jnp.where((i0 >> 5) == m, outlet_of, 0.0).astype(BF)
        scat[m * 128 : (m + 1) * 128, :] = jnp.where((i1 >> 5) == m, link_t, 0.0).astype(BF)
    outlet_bf = outlet_of.astype(BF)
    joined = mm_nt(outlet_bf, link_of.astype(BF))
    perm[...] = jnp.where((i0 >> 5) == (i1 >> 5), joined, 0.0).astype(BF)
    cls_c = jnp.broadcast_to(cls_ref[...].astype(F32), (128, 128)).T
    cls_o = mm(outlet_bf, cls_c.astype(BF))
    for k in range(classes):
        hit_c = onehot(cls_c == float(k)).astype(BF)
        hit_o = onehot(cls_o == float(k)).astype(BF)
        for a in range(2):
            mask_o[k, :, a * 128 : (a + 1) * 128] = hit_o
            for b in range(2):
                mask_c[k, b * 128 : (b + 1) * 128, a * 128 : (a + 1) * 128] = hit_c

    @pl.when(o == 0)
    def _():
        inbox[...] = jnp.zeros_like(inbox)

    def route(rows):
        total = mm(rows * mask_o[0], toep_t[0:LANES, :])
        for k in range(1, classes):
            total = total + mm(rows * mask_o[k], toep_t[k * LANES : (k + 1) * LANES, :])
        return total

    def group(g, c):
        pltpu.make_async_copy(recv.at[g], recv.at[g], rsem.at[g]).wait()
        got = recv[g].reshape(slots, LANES)
        lat[...] = mm(w_hi[...], got) + mm(w_lo[...], got)
        base = mm(out_sel[...], lat[...].astype(BF)).astype(BF)
        base_out[...] = route(base)

        @pl.when(o == 0)
        def _():
            outbox[g] = base_out[...].astype(BF)

        @pl.when(o > 0)
        def _():
            pltpu.make_async_copy(inbox.at[g], inbox.at[g], crsem.at[g]).wait()
            moved = mm(perm[...], inbox[g]).astype(BF)
            outbox[g] = (base_out[...] + route(moved)).astype(BF)

        @pl.when(o < orders - 1)
        def _():
            pltpu.make_async_remote_copy(
                src_ref=outbox.at[g],
                dst_ref=inbox.at[g],
                send_sem=cssem.at[g],
                recv_sem=crsem.at[g],
                device_id=(r, nxt),
                device_id_type=MESH,
            ).start()

        lat[...] = lat[...] + mm(scat[...], inbox[g])

        def pair(h, c):
            entering = lat[pl.ds(pl.multiple_of(h * 256, 256), 256), :].astype(BF)
            total = mm_nt(toep[:, 0:LANES], entering * mask_c[0])
            for k in range(1, classes):
                at = k * LANES
                total = total + mm_nt(toep[:, at : at + LANES], entering * mask_c[k])
            for m in range(2):
                first = g * MG + h * 2 + m
                out32[pl.ds(first, hours, stride=members), :] = total[
                    0:hours, m * 128 : (m + 1) * 128
                ]
            return c

        return lax.fori_loop(0, 2, pair, c)

    lax.fori_loop(0, groups, group, 0)

    block = hours // 10

    def finish(b, c):
        t = b * block
        rows = block * members
        part = out32[pl.ds(pl.multiple_of(t * members, rows), rows), :]
        out_ref[pl.ds(t, block)] = part.reshape(block, members, 128).astype(BF)
        return c

    lax.fori_loop(0, 10, finish, 0)

    def drain(g, c):
        sent = send.at[g, pl.ds(0, regions - 1)]
        pltpu.make_async_copy(sent, sent, ssem.at[g]).wait()

        @pl.when(o < orders - 1)
        def _():
            pltpu.make_async_copy(outbox.at[g], outbox.at[g], cssem.at[g]).wait()

        return c

    lax.fori_loop(0, groups, drain, 0)


def local(
    regions,
    orders,
    runoff,
    send_rows,
    remap_index,
    remap_weight,
    class_id,
    kernel_shape,
    kernel_rate,
    outlets,
    incidence,
):
    hours, members, rows = runoff.shape
    reaches = remap_index.shape[0]
    classes = kernel_shape.shape[0]
    panel = outlets.shape[2]
    groups = members // MG
    slots = regions * MG * 4
    sizes = (hours, members, regions, orders, reaches, classes, panel)
    vmem = pl.BlockSpec(memory_space=pltpu.VMEM)
    return pl.pallas_call(
        functools.partial(kernel, sizes),
        out_shape=jax.ShapeDtypeStruct((hours, members, reaches), BF),
        in_specs=[vmem] * 9,
        out_specs=vmem,
        scratch_shapes=[
            pltpu.VMEM((MG * rows, LANES), BF),
            pltpu.VMEM((groups, regions, MG * 4, LANES), BF),
            pltpu.VMEM((groups, regions, MG * 4, LANES), BF),
            pltpu.VMEM((groups, MG * panel, LANES), BF),
            pltpu.VMEM((groups, MG * panel, LANES), BF),
            pltpu.VMEM((MG * reaches, LANES), F32),
            pltpu.VMEM((MG * panel, LANES), F32),
            pltpu.VMEM((hours * members, reaches), F32),
            pltpu.VMEM((slots, MG * rows), BF),
            pltpu.VMEM((MG * reaches, slots), BF),
            pltpu.VMEM((MG * reaches, slots), BF),
            pltpu.VMEM((MG * panel, MG * reaches), BF),
            pltpu.VMEM((MG * panel, MG * panel), BF),
            pltpu.VMEM((MG * reaches, MG * panel), BF),
            pltpu.VMEM((classes, MG * panel, LANES), BF),
            pltpu.VMEM((classes, 2 * reaches, LANES), BF),
            pltpu.VMEM((LANES, classes * LANES), BF),
            pltpu.VMEM((classes * LANES, LANES), BF),
            pltpu.SemaphoreType.DMA((groups,)),
            pltpu.SemaphoreType.DMA((groups,)),
            pltpu.SemaphoreType.DMA((groups,)),
            pltpu.SemaphoreType.DMA((groups,)),
        ],
        compiler_params=pltpu.CompilerParams(
            collective_id=0, has_side_effects=True, vmem_limit_bytes=56 << 20
        ),
        name="route_levels",
    )(
        jnp.transpose(runoff, (1, 2, 0)).reshape(members * rows, hours),
        send_rows.reshape(1, -1),
        remap_index.T,
        remap_weight.T,
        class_id.reshape(1, -1),
        kernel_shape,
        kernel_rate.reshape(1, -1),
        outlets.reshape(1, -1),
        incidence.reshape(panel, reaches),
    )


def solution(mesh):
    return jax.shard_map(
        functools.partial(local, mesh.shape["region"], mesh.shape["order"]),
        mesh=mesh,
        in_specs=(
            P(None, None, ("region", "order")),
            P("region", "order", None),
            P(("region", "order"), None),
            P(("region", "order"), None),
            P(("region", "order"), None),
            P(),
            P(),
            P("region", "order", None),
            P("region", "order", None, None),
        ),
        out_specs=P(None, None, ("region", "order")),
        check_vma=False,
    )
```

profile of v0, /device:TPU:25, one launch (start us, length us, event | category | flops | bytes accessed | tf_op | source)
XLA Modules:
  0.0 80.1 jit_solution(8335056817703099780)
XLA Ops:
  0.0 76.9 %route_levels.1 = bf16[240,32,128]{2,1,0:T(8,128)(2,1)} custom-call(f32[1024,240]{1,0:T(8,128)} %bitcast.10, s32[1,128]{1,0:T(1,128)} %bitcast.14, s32[4,128]{1,0:T(4,128)} %bitcast.12, f32[4,128]{1,0:T(4,128)} %bitcast.13, s32[1,128]{1,0:T(1,128)} %bitcast.15, f32[8,240]{1,0:T(8,128)} %shape_ref.1, f32[1,8]{1,0:T(1,128)} %bitcast.16, s32[1,32]{1,0:T(1,128)} %bitcast.17, ...), custom_call_target="tpu_custom_call" | custom-call | tf_op jit(solution)/shard_map/route_levels/pallas_call | solution.py:281
  76.9 3.2 %copy.11 = bf16[240,32,128]{2,1,0:T(8,128)(2,1)} copy(bf16[240,32,128]{2,1,0:T(8,128)(2,1)} %route_levels.1) | data formatting | bytes 3932160
where the time goes:
time: 80.2 us; the launch traced here: 80.1 us
  Pallas kernels  76.9 us (96%)
  local copies, waits for them, and re-layouts  3.15 us (4%)
    pallas_call x1, Pallas kernels, local(): pl.pallas_call(functools.partial(kernel, sizes), out_shape=jax.ShapeDtype...  76.9 us
    unnamed x1, local copies, waits for them, and re-layouts  3.15 us

commit v1 on v0

--- a/solution.py
+++ b/solution.py
@@ -32,16 +32,18 @@
 
 def kernel(
     sizes,
-    x_ref,
-    send_rows_ref,
-    idx_ref,
-    w_ref,
-    cls_ref,
-    shape_ref,
-    rate_ref,
-    outlets_ref,
-    inc_ref,
-    out_ref,
+    *refs,
+):
+    given, out32, held = refs[:9], refs[9], refs[10:19]
+    route_body(sizes, given, held, out32, *refs[19:])
+
+
+def route_body(
+    sizes,
+    given,
+    held,
+    out32,
+    insem,
     xb,
     send,
     recv,
@@ -49,11 +51,11 @@
     outbox,
     lat,
     base_out,
-    out32,
     sel,
     w_hi,
     w_lo,
-    out_sel,
+    wo_hi,
+    wo_lo,
     perm,
     scat,
     mask_o,
@@ -66,6 +68,12 @@
     crsem,
 ):
     hours, members, regions, orders, reaches, classes, panel = sizes
+    x_ref, send_rows_ref, idx_ref, w_ref, cls_ref, shape_ref, rate_ref, outlets_ref, inc_ref = held
+    loads = [
+        pltpu.make_async_copy(given[i], held[i], insem.at[i]) for i in range(len(held))
+    ]
+    for load in loads:
+        load.start()
     groups = members // MG
     slots = send.shape[2] * regions
     r = lax.axis_index("region")
@@ -87,11 +95,13 @@
     n0 = iota((slots, 128), 0)
     c1 = iota((slots, 128), 1)
     spread = onehot(c1 == (n0 >> 4) * 4 + (n0 & 3)).astype(BF)
+    loads[1].wait()
     row_hit = onehot(send_rows_ref[...] == (iota((128, 128), 0) & 31)).astype(BF)
     picked = mm_nt(spread, row_hit)
     sel[...] = jnp.where(((n0 >> 2) & 3) == (c1 >> 5), picked, 0.0).astype(BF)
     xb[:, 128:LANES] = jnp.zeros((xb.shape[0], LANES - 128), BF)
 
+    loads[0].wait()
     pl.semaphore_wait(barrier, regions + 1)
 
     def dispatch(g, c):
@@ -116,6 +126,9 @@
         return lax.fori_loop(1, regions, push, c)
 
     lax.fori_loop(0, groups, dispatch, 0)
+
+    for load in loads[2:]:
+        load.wait()
 
     diag = iota((classes, classes), 0) == iota((classes, classes), 1)
     rate = jnp.sum(
@@ -161,9 +174,11 @@
     link_of = mm(copies, inc_ref[...].astype(F32).astype(BF))
     link_t = link_of.T
     for m in range(MG):
-        out_sel[:, m * 128 : (m + 1) * 128] = jnp.where((i0 >> 5) == m, outlet_of, 0.0).astype(BF)
         scat[m * 128 : (m + 1) * 128, :] = jnp.where((i1 >> 5) == m, link_t, 0.0).astype(BF)
     outlet_bf = outlet_of.astype(BF)
+    own = ((iota((MG * panel, slots), 1) >> 2) & 3) == (iota((MG * panel, slots), 0) >> 5)
+    wo_hi[...] = jnp.where(own, mm(outlet_bf, high), 0.0).astype(BF)
+    wo_lo[...] = jnp.where(own, mm(outlet_bf, low), 0.0).astype(BF)
     joined = mm_nt(outlet_bf, link_of.astype(BF))
     perm[...] = jnp.where((i0 >> 5) == (i1 >> 5), joined, 0.0).astype(BF)
     cls_c = jnp.broadcast_to(cls_ref[...].astype(F32), (128, 128)).T
@@ -176,10 +191,6 @@
             for b in range(2):
                 mask_c[k, b * 128 : (b + 1) * 128, a * 128 : (a + 1) * 128] = hit_c
 
-    @pl.when(o == 0)
-    def _():
-        inbox[...] = jnp.zeros_like(inbox)
-
     def route(rows):
         total = mm(rows * mask_o[0], toep_t[0:LANES, :])
         for k in range(1, classes):
@@ -189,22 +200,8 @@
     def group(g, c):
         pltpu.make_async_copy(recv.at[g], recv.at[g], rsem.at[g]).wait()
         got = recv[g].reshape(slots, LANES)
-        lat[...] = mm(w_hi[...], got) + mm(w_lo[...], got)
-        base = mm(out_sel[...], lat[...].astype(BF)).astype(BF)
-        base_out[...] = route(base)
-
-        @pl.when(o == 0)
-        def _():
-            outbox[g] = base_out[...].astype(BF)
-
-        @pl.when(o > 0)
-        def _():
-            pltpu.make_async_copy(inbox.at[g], inbox.at[g], crsem.at[g]).wait()
-            moved = mm(perm[...], inbox[g]).astype(BF)
-            outbox[g] = (base_out[...] + route(moved)).astype(BF)
-
-        @pl.when(o < orders - 1)
-        def _():
+
+        def pass_on():
             pltpu.make_async_remote_copy(
                 src_ref=outbox.at[g],
                 dst_ref=inbox.at[g],
@@ -214,7 +211,28 @@
                 device_id_type=MESH,
             ).start()
 
-        lat[...] = lat[...] + mm(scat[...], inbox[g])
+        @pl.when(o < orders - 1)
+        def _():
+            base_out[...] = route((mm(wo_hi[...], got) + mm(wo_lo[...], got)).astype(BF))
+
+        @pl.when(o == 0)
+        def _():
+            outbox[g] = base_out[...].astype(BF)
+            pass_on()
+
+        lat[...] = mm(w_hi[...], got) + mm(w_lo[...], got)
+
+        @pl.when(o > 0)
+        def _():
+            pltpu.make_async_copy(inbox.at[g], inbox.at[g], crsem.at[g]).wait()
+
+            @pl.when(o < orders - 1)
+            def _():
+                moved = mm(perm[...], inbox[g]).astype(BF)
+                outbox[g] = (base_out[...] + route(moved)).astype(BF)
+                pass_on()
+
+            lat[...] = lat[...] + mm(scat[...], inbox[g])
 
         def pair(h, c):
             entering = lat[pl.ds(pl.multiple_of(h * 256, 256), 256), :].astype(BF)
@@ -232,17 +250,6 @@
         return lax.fori_loop(0, 2, pair, c)
 
     lax.fori_loop(0, groups, group, 0)
-
-    block = hours // 10
-
-    def finish(b, c):
-        t = b * block
-        rows = block * members
-        part = out32[pl.ds(pl.multiple_of(t * members, rows), rows), :]
-        out_ref[pl.ds(t, block)] = part.reshape(block, members, 128).astype(BF)
-        return c
-
-    lax.fori_loop(0, 10, finish, 0)
 
     def drain(g, c):
         sent = send.at[g, pl.ds(0, regions - 1)]
@@ -277,13 +284,25 @@
     groups = members // MG
     slots = regions * MG * 4
     sizes = (hours, members, regions, orders, reaches, classes, panel)
-    vmem = pl.BlockSpec(memory_space=pltpu.VMEM)
-    return pl.pallas_call(
+    given = (
+        jnp.transpose(runoff, (1, 2, 0)).reshape(members * rows, hours),
+        send_rows.reshape(1, -1),
+        remap_index.T,
+        remap_weight.T,
+        class_id.reshape(1, -1),
+        kernel_shape,
+        kernel_rate.reshape(1, -1),
+        outlets.reshape(1, -1),
+        incidence.reshape(panel, reaches),
+    )
+    flat = pl.pallas_call(
         functools.partial(kernel, sizes),
-        out_shape=jax.ShapeDtypeStruct((hours, members, reaches), BF),
-        in_specs=[vmem] * 9,
-        out_specs=vmem,
-        scratch_shapes=[
+        out_shape=pltpu.VMEM((hours * members, reaches), F32),
+        in_specs=[pl.BlockSpec(memory_space=pltpu.HBM)] * len(given),
+        out_specs=pl.BlockSpec(memory_space=pltpu.VMEM),
+        scratch_shapes=[pltpu.VMEM(a.shape, a.dtype) for a in given]
+        + [
+            pltpu.SemaphoreType.DMA((len(given),)),
             pltpu.VMEM((MG * rows, LANES), BF),
             pltpu.VMEM((groups, regions, MG * 4, LANES), BF),
             pltpu.VMEM((groups, regions, MG * 4, LANES), BF),
@@ -291,11 +310,11 @@
             pltpu.VMEM((groups, MG * panel, LANES), BF),
             pltpu.VMEM((MG * reaches, LANES), F32),
             pltpu.VMEM((MG * panel, LANES), F32),
-            pltpu.VMEM((hours * members, reaches), F32),
             pltpu.VMEM((slots, MG * rows), BF),
             pltpu.VMEM((MG * reaches, slots), BF),
             pltpu.VMEM((MG * reaches, slots), BF),
-            pltpu.VMEM((MG * panel, MG * reaches), BF),
+            pltpu.VMEM((MG * panel, slots), BF),
+            pltpu.VMEM((MG * panel, slots), BF),
             pltpu.VMEM((MG * panel, MG * panel), BF),
             pltpu.VMEM((MG * reaches, MG * panel), BF),
             pltpu.VMEM((classes, MG * panel, LANES), BF),
@@ -311,17 +330,8 @@
             collective_id=0, has_side_effects=True, vmem_limit_bytes=56 << 20
         ),
         name="route_levels",
-    )(
-        jnp.transpose(runoff, (1, 2, 0)).reshape(members * rows, hours),
-        send_rows.reshape(1, -1),
-        remap_index.T,
-        remap_weight.T,
-        class_id.reshape(1, -1),
-        kernel_shape,
-        kernel_rate.reshape(1, -1),
-        outlets.reshape(1, -1),
-        incidence.reshape(panel, reaches),
-    )
+    )(*given)
+    return flat.reshape(hours, members, reaches).astype(BF)
 
 
 def solution(mesh):

time: 80.2 us -> 75 us (0.935)
  Pallas kernels: 76.9 us -> 73.4 us
  local copies, waits for them, and re-layouts: 3.15 us -> 0 us
  other arithmetic: 0 us -> 1.46 us
    pallas_call x1, Pallas kernels: 76.9 us -> 73.4 us  [local(): pl.pallas_call(functools.partial(kernel, sizes), out_shape=pltpu.VMEM((ho...]
    unnamed x1 -> x0, local copies, waits for them, and re-layouts: 3.15 us -> none
    convert_element_type x0 -> x1, other arithmetic: none -> 1.46 us  [local(): return flat.reshape(hours, members, reaches).astype(BF)]
where the time goes in v1:
time: 75 us; the launch traced here: 74.9 us
  Pallas kernels  73.4 us (98%)
  other arithmetic  1.46 us (2%)
    pallas_call x1, Pallas kernels, local(): pl.pallas_call(functools.partial(kernel, sizes), out_shape=pltpu.VMEM((ho...  73.4 us

profile of v1, /device:TPU:25, one launch (start us, length us, event | category | flops | bytes accessed | tf_op | source)
XLA Modules:
  0.0 74.9 jit_solution(16904739166268930476)
XLA Ops:
  0.0 73.4 %route_levels.1 = f32[7680,128]{1,0:T(8,128)S(1)} custom-call(f32[1024,240]{1,0:T(8,128)} %bitcast.11, s32[1,128]{1,0:T(1,128)} %bitcast.15, s32[4,128]{1,0:T(4,128)} %bitcast.13, f32[4,128]{1,0:T(4,128)} %bitcast.14, s32[1,128]{1,0:T(1,128)} %bitcast.16, f32[8,240]{1,0:T(8,128)} %refs_5_.1, f32[1,8]{1,0:T(1,128)} %bitcast.17, s32[1,32]{1,0:T(1,128)} %bitcast.18, ...), custom_call_target="tpu_custom_call" | custom-call | tf_op jit(solution)/shard_map/route_levels/pallas_call | solution.py:298
  73.4 1.5 %convert_element_type.6 = bf16[7680,128]{1,0:T(8,128)(2,1)} convert(f32[7680,128]{1,0:T(8,128)S(1)} %route_levels.1) | non-fusion elementwise | flops 983040 | bytes 5898240 | tf_op jit(solution)/shard_map/convert_element_type | solution.py:334

commit v2 on v1

--- a/solution.py
+++ b/solution.py
@@ -9,8 +9,12 @@
 
 MESH = pl.DeviceIdType.MESH
 BF = jnp.bfloat16
+NX, NZ = 4, 8
 F32 = jnp.float32
 LANES = 256
+AHEAD = 2
+PICK = 2
+LAG = 4
 MG = 4
 
 
@@ -44,8 +48,12 @@
     held,
     out32,
     insem,
-    xb,
-    send,
+    own,
+    near1,
+    near2,
+    meta,
+    send_n,
+    send_f,
     recv,
     inbox,
     outbox,
@@ -62,7 +70,14 @@
     mask_c,
     toep,
     toep_t,
-    ssem,
+    msend,
+    mrecv,
+    s1s,
+    s1r,
+    s2s,
+    s2r,
+    nsem,
+    fsem,
     rsem,
     cssem,
     crsem,
@@ -75,58 +90,81 @@
     for load in loads:
         load.start()
     groups = members // MG
-    slots = send.shape[2] * regions
+    slots = regions * MG * 4
     r = lax.axis_index("region")
     o = lax.axis_index("order")
+    x = r // NZ
+    z = lax.rem(r, NZ)
     nxt = lax.rem(o + 1, orders)
     prv = lax.rem(o + orders - 1, orders)
 
+    def at(dx, dz):
+        return (lax.rem(x + dx + NX, NX) * NZ + lax.rem(z + dz + NZ, NZ), o)
+
     barrier = pltpu.get_barrier_semaphore()
 
-    def greet(d, c):
-        peer = lax.rem(r + d, regions)
-        pl.semaphore_signal(barrier, inc=1, device_id=(peer, o), device_id_type=MESH)
+    def greet(n, c):
+        peer = at(n // 5, lax.rem(n, 5) + NZ - 2)
+        pl.semaphore_signal(barrier, inc=1, device_id=peer, device_id_type=MESH)
         return c
 
-    lax.fori_loop(1, regions, greet, 0)
-    pl.semaphore_signal(barrier, inc=1, device_id=(r, nxt), device_id_type=MESH)
+    lax.fori_loop(0, 2, greet, 0)
+    lax.fori_loop(3, NX * 5, greet, 0)
     pl.semaphore_signal(barrier, inc=1, device_id=(r, prv), device_id_type=MESH)
 
-    n0 = iota((slots, 128), 0)
-    c1 = iota((slots, 128), 1)
-    spread = onehot(c1 == (n0 >> 4) * 4 + (n0 & 3)).astype(BF)
-    loads[1].wait()
-    row_hit = onehot(send_rows_ref[...] == (iota((128, 128), 0) & 31)).astype(BF)
-    picked = mm_nt(spread, row_hit)
-    sel[...] = jnp.where(((n0 >> 2) & 3) == (c1 >> 5), picked, 0.0).astype(BF)
-    xb[:, 128:LANES] = jnp.zeros((xb.shape[0], LANES - 128), BF)
-
+    own[:, :, 128:LANES] = jnp.zeros((groups, MG * 32, LANES - 128), BF)
     loads[0].wait()
-    pl.semaphore_wait(barrier, regions + 1)
-
-    def dispatch(g, c):
+
+    def cast(g, c):
         rows = MG * 32
         start = pl.multiple_of(g * rows, rows)
-        xb[:, 0:hours] = x_ref[pl.ds(start, rows), :].astype(BF)
-        send[g] = mm(sel[...], xb[...]).astype(BF).reshape(send.shape[1:])
-        pltpu.make_async_copy(send.at[g, r], recv.at[g, r], rsem.at[g]).start()
-
-        def push(d, c):
-            peer = lax.rem(r + d, regions)
+        own[g, :, 0:hours] = x_ref[pl.ds(start, rows), :].astype(BF)
+        return c
+
+    lax.fori_loop(0, groups, cast, 0)
+    loads[1].wait()
+    meta[2] = send_rows_ref[...]
+    pl.semaphore_wait(barrier, NX * 5)
+
+    def step1(g):
+        for way in range(2):
             pltpu.make_async_remote_copy(
-                src_ref=send.at[g, peer],
-                dst_ref=recv.at[g, r],
-                send_sem=ssem.at[g],
-                recv_sem=rsem.at[g],
-                device_id=(peer, o),
+                src_ref=own.at[g],
+                dst_ref=near1.at[g, way],
+                send_sem=s1s.at[g, way],
+                recv_sem=s1r.at[g, way],
+                device_id=at(0, 1 - 2 * way),
                 device_id_type=MESH,
             ).start()
-            return c
-
-        return lax.fori_loop(1, regions, push, c)
-
-    lax.fori_loop(0, groups, dispatch, 0)
-
+
+    def step2(g):
+        for way in range(2):
+            pltpu.make_async_copy(near1.at[g, way], near1.at[g, way], s1r.at[g, way]).wait()
+            pltpu.make_async_remote_copy(
+                src_ref=near1.at[g, way],
+                dst_ref=near2.at[g, way],
+                send_sem=s2s.at[g, way],
+                recv_sem=s2r.at[g, way],
+                device_id=at(0, 1 - 2 * way),
+                device_id_type=MESH,
+            ).start()
+
+    step1(0)
+    tell = [
+        pltpu.make_async_remote_copy(
+            src_ref=send_rows_ref,
+            dst_ref=meta.at[2 + dz],
+            send_sem=msend.at[n],
+            recv_sem=mrecv.at[2 + dz],
+            device_id=at(0, dz),
+            device_id_type=MESH,
+        )
+        for n, dz in enumerate((1, -1, 2, -2))
+    ]
+    for copy in tell:
+        copy.start()
+    for g in range(1, AHEAD):
+        step1(g)
     for load in loads[2:]:
         load.wait()
 
@@ -153,7 +191,9 @@
 
     lax.fori_loop(0, classes, table, 0)
 
-    pos = (n0 >> 4) * 4 + (n0 & 3)
+    n0 = iota((slots, 128), 0)
+    source = (n0 >> 7) * NZ + ((z + 2 + NZ - ((n0 >> 4) & 7)) & 7)
+    pos = source * 4 + (n0 & 3)
     weights_t = jnp.zeros((slots, 128), F32)
     for j in range(4):
         weights_t = weights_t + jnp.where(idx_ref[j : j + 1, :] == pos, w_ref[j : j + 1, :], 0.0)
@@ -176,9 +216,9 @@
     for m in range(MG):
         scat[m * 128 : (m + 1) * 128, :] = jnp.where((i1 >> 5) == m, link_t, 0.0).astype(BF)
     outlet_bf = outlet_of.astype(BF)
-    own = ((iota((MG * panel, slots), 1) >> 2) & 3) == (iota((MG * panel, slots), 0) >> 5)
-    wo_hi[...] = jnp.where(own, mm(outlet_bf, high), 0.0).astype(BF)
-    wo_lo[...] = jnp.where(own, mm(outlet_bf, low), 0.0).astype(BF)
+    mine = ((iota((MG * panel, slots), 1) >> 2) & 3) == (iota((MG * panel, slots), 0) >> 5)
+    wo_hi[...] = jnp.where(mine, mm(outlet_bf, high), 0.0).astype(BF)
+    wo_lo[...] = jnp.where(mine, mm(outlet_bf, low), 0.0).astype(BF)
     joined = mm_nt(outlet_bf, link_of.astype(BF))
     perm[...] = jnp.where((i0 >> 5) == (i1 >> 5), joined, 0.0).astype(BF)
     cls_c = jnp.broadcast_to(cls_ref[...].astype(F32), (128, 128)).T
@@ -191,13 +231,72 @@
             for b in range(2):
                 mask_c[k, b * 128 : (b + 1) * 128, a * 128 : (a + 1) * 128] = hit_c
 
+    for copy in tell:
+        copy.wait_recv()
+    k0 = iota((160, 128), 0)
+    k1 = iota((160, 128), 1)
+    part = k0 >> 6
+    for e in range(5):
+        way = 1 if e < 2 else 0
+        ahead = part * (1 - 2 * way)
+        to_x = jnp.where(part == 2, (x + 2 * way + ((k0 >> 4) & 3)) & 3, (k0 >> 4) & 3)
+        to_z = (z + ahead + NZ) & 7
+        spread = onehot(k1 == (to_x * NZ + to_z) * 4 + (k0 & 3)).astype(BF)
+        row_hit = onehot(meta[e] == (iota((128, 128), 0) & 31)).astype(BF)
+        picked = mm_nt(spread, row_hit)
+        sel[e] = jnp.where(((k0 >> 2) & 3) == (k1 >> 5), picked, 0.0).astype(BF)
+
+    def select(g):
+        for way in range(2):
+            pltpu.make_async_copy(near2.at[g, way], near2.at[g, way], s2r.at[g, way]).wait()
+        held_blocks = (near2[g, 1], near1[g, 1], own[g], near1[g, 0], near2[g, 0])
+        for e in (0, 4, 1, 2, 3):
+            outer = e == 0 or e == 4
+            taken = mm(sel[e] if outer else sel[e, 0:64, :], held_blocks[e]).astype(BF)
+            send_n[g, :, e] = taken[0:64].reshape(NX, MG * 4, LANES)
+            if outer:
+                way = 0 if e == 4 else 1
+                send_f[g, way] = taken[64:160].reshape(6, MG * 4, LANES)
+
+                def far(n, c, way=way):
+                    two = n // 4
+                    dx = n + two * (2 * way)
+                    dz = (1 + two) * (1 - 2 * way)
+                    to_x = jnp.where(two == 1, lax.rem(x + dx, NX), n)
+                    peer = (to_x * NZ + lax.rem(z + dz + NZ, NZ), o)
+                    into = jnp.where(two == 1, 6, 5 + 2 * way)
+                    pltpu.make_async_remote_copy(
+                        src_ref=send_f.at[g, way, n],
+                        dst_ref=recv.at[g, x, into],
+                        send_sem=fsem.at[g],
+                        recv_sem=rsem.at[g],
+                        device_id=peer,
+                        device_id_type=MESH,
+                    ).start()
+                    return c
+
+                lax.fori_loop(0, 6, far, 0)
+
+        def near(d, c):
+            to_x = lax.rem(x + d, NX)
+            pltpu.make_async_remote_copy(
+                src_ref=send_n.at[g, to_x],
+                dst_ref=recv.at[g, x, pl.ds(0, 5)],
+                send_sem=nsem.at[g],
+                recv_sem=rsem.at[g],
+                device_id=(to_x * NZ + z, o),
+                device_id_type=MESH,
+            ).start()
+            return c
+
+        lax.fori_loop(1, NX, near, 0)
+        pltpu.make_async_copy(send_n.at[g, x], recv.at[g, x, pl.ds(0, 5)], rsem.at[g]).start()
+
     def route(rows):
-        total = mm(rows * mask_o[0], toep_t[0:LANES, :])
-        for k in range(1, classes):
-            total = total + mm(rows * mask_o[k], toep_t[k * LANES : (k + 1) * LANES, :])
-        return total
-
-    def group(g, c):
+        wide = jnp.concatenate([rows * mask_o[k] for k in range(classes)], axis=1)
+        return mm(wide, toep_t[...])
+
+    def group(g):
         pltpu.make_async_copy(recv.at[g], recv.at[g], rsem.at[g]).wait()
         got = recv[g].reshape(slots, LANES)
 
@@ -236,10 +335,8 @@
 
         def pair(h, c):
             entering = lat[pl.ds(pl.multiple_of(h * 256, 256), 256), :].astype(BF)
-            total = mm_nt(toep[:, 0:LANES], entering * mask_c[0])
-            for k in range(1, classes):
-                at = k * LANES
-                total = total + mm_nt(toep[:, at : at + LANES], entering * mask_c[k])
+            wide = jnp.concatenate([entering * mask_c[k] for k in range(classes)], axis=1)
+            total = mm_nt(toep[...], wide)
             for m in range(2):
                 first = g * MG + h * 2 + m
                 out32[pl.ds(first, hours, stride=members), :] = total[
@@ -247,13 +344,39 @@
                 ]
             return c
 
-        return lax.fori_loop(0, 2, pair, c)
-
-    lax.fori_loop(0, groups, group, 0)
+        lax.fori_loop(0, 2, pair, 0)
+
+    def turn(i, c):
+        @pl.when(i < groups - AHEAD)
+        def _():
+            step1(i + AHEAD)
+
+        @pl.when(i < groups)
+        def _():
+            step2(i)
+
+        @pl.when(jnp.logical_and(i >= PICK, i < groups + PICK))
+        def _():
+            select(i - PICK)
+
+        @pl.when(i >= LAG)
+        def _():
+            group(i - LAG)
+
+        return c
+
+    lax.fori_loop(0, groups + LAG, turn, 0)
+
+    for copy in tell:
+        copy.wait_send()
 
     def drain(g, c):
-        sent = send.at[g, pl.ds(0, regions - 1)]
-        pltpu.make_async_copy(sent, sent, ssem.at[g]).wait()
+        for way in range(2):
+            pltpu.make_async_copy(own.at[g], own.at[g], s1s.at[g, way]).wait()
+            pltpu.make_async_copy(near1.at[g, way], near1.at[g, way], s2s.at[g, way]).wait()
+        sent = send_n.at[g, pl.ds(0, NX - 1)]
+        pltpu.make_async_copy(sent, sent, nsem.at[g]).wait()
+        pltpu.make_async_copy(send_f.at[g], send_f.at[g], fsem.at[g]).wait()
 
         @pl.when(o < orders - 1)
         def _():
@@ -303,14 +426,18 @@
         scratch_shapes=[pltpu.VMEM(a.shape, a.dtype) for a in given]
         + [
             pltpu.SemaphoreType.DMA((len(given),)),
-            pltpu.VMEM((MG * rows, LANES), BF),
-            pltpu.VMEM((groups, regions, MG * 4, LANES), BF),
-            pltpu.VMEM((groups, regions, MG * 4, LANES), BF),
+            pltpu.VMEM((groups, MG * rows, LANES), BF),
+            pltpu.VMEM((groups, 2, MG * rows, LANES), BF),
+            pltpu.VMEM((groups, 2, MG * rows, LANES), BF),
+            pltpu.VMEM((5, 1, 128), jnp.int32),
+            pltpu.VMEM((groups, NX, 5, MG * 4, LANES), BF),
+            pltpu.VMEM((groups, 2, 6, MG * 4, LANES), BF),
+            pltpu.VMEM((groups, NX, NZ, MG * 4, LANES), BF),
             pltpu.VMEM((groups, MG * panel, LANES), BF),
             pltpu.VMEM((groups, MG * panel, LANES), BF),
             pltpu.VMEM((MG * reaches, LANES), F32),
             pltpu.VMEM((MG * panel, LANES), F32),
-            pltpu.VMEM((slots, MG * rows), BF),
+            pltpu.VMEM((5, 160, MG * rows), BF),
             pltpu.VMEM((MG * reaches, slots), BF),
             pltpu.VMEM((MG * reaches, slots), BF),
             pltpu.VMEM((MG * panel, slots), BF),
@@ -321,6 +448,13 @@
             pltpu.VMEM((classes, 2 * reaches, LANES), BF),
             pltpu.VMEM((LANES, classes * LANES), BF),
             pltpu.VMEM((classes * LANES, LANES), BF),
+            pltpu.SemaphoreType.DMA((4,)),
+            pltpu.SemaphoreType.DMA((5,)),
+            pltpu.SemaphoreType.DMA((groups, 2)),
+            pltpu.SemaphoreType.DMA((groups, 2)),
+            pltpu.SemaphoreType.DMA((groups, 2)),
+            pltpu.SemaphoreType.DMA((groups, 2)),
+            pltpu.SemaphoreType.DMA((groups,)),
             pltpu.SemaphoreType.DMA((groups,)),
             pltpu.SemaphoreType.DMA((groups,)),
             pltpu.SemaphoreType.DMA((groups,)),

time: 75 us -> 72 us (0.960)
  Pallas kernels: 73.4 us -> 70.4 us
    pallas_call x1, Pallas kernels: 73.4 us -> 70.4 us  [local(): pl.pallas_call(functools.partial(kernel, sizes), out_shape=pltpu.VMEM((ho...]
where the time goes in v2:
time: 72 us; the launch traced here: 71.9 us
  Pallas kernels  70.4 us (98%)
  other arithmetic  1.46 us (2%)
    pallas_call x1, Pallas kernels, local(): pl.pallas_call(functools.partial(kernel, sizes), out_shape=pltpu.VMEM((ho...  70.4 us
    convert_element_type x1, other arithmetic, local(): return flat.reshape(hours, members, reaches).astype(BF)  1.46 us

profile of v2, /device:TPU:25, one launch (start us, length us, event | category | flops | bytes accessed | tf_op | source)
XLA Modules:
  0.0 71.9 jit_solution(15093547345936018522)
XLA Ops:
  0.0 70.4 %route_levels.1 = f32[7680,128]{1,0:T(8,128)S(1)} custom-call(f32[1024,240]{1,0:T(8,128)} %bitcast.11, s32[1,128]{1,0:T(1,128)} %bitcast.15, s32[4,128]{1,0:T(4,128)} %bitcast.13, f32[4,128]{1,0:T(4,128)} %bitcast.14, s32[1,128]{1,0:T(1,128)} %bitcast.16, f32[8,240]{1,0:T(8,128)} %refs_5_.1, f32[1,8]{1,0:T(1,128)} %bitcast.17, s32[1,32]{1,0:T(1,128)} %bitcast.18, ...), custom_call_target="tpu_custom_call" | custom-call | tf_op jit(solution)/shard_map/route_levels/pallas_call | solution.py:421
  70.4 1.5 %convert_element_type.6 = bf16[7680,128]{1,0:T(8,128)(2,1)} convert(f32[7680,128]{1,0:T(8,128)S(1)} %route_levels.1) | non-fusion elementwise | flops 983040 | bytes 5898240 | tf_op jit(solution)/shard_map/convert_element_type | solution.py:468

commit v3 on v2

--- a/solution.py
+++ b/solution.py
@@ -13,6 +13,7 @@
 F32 = jnp.float32
 LANES = 256
 AHEAD = 2
+SPARE = 14
 PICK = 2
 LAG = 4
 MG = 4
@@ -186,7 +187,10 @@
         turned = jnp.where(later, turned, 0.0)
         at = pl.multiple_of(k * LANES, LANES)
         toep_t[pl.ds(at, LANES), :] = turned.astype(BF)
-        toep[:, pl.ds(at, LANES)] = turned.T.astype(BF)
+        flipped = turned.T.astype(BF)
+        here = pl.multiple_of(k * 128, 128)
+        toep[:, pl.ds(here, 128)] = flipped[:, 0:128]
+        toep[:, pl.ds(here + classes * 128, 128)] = flipped[:, 128:LANES]
         return c
 
     lax.fori_loop(0, classes, table, 0)
@@ -228,8 +232,7 @@
         hit_o = onehot(cls_o == float(k)).astype(BF)
         for a in range(2):
             mask_o[k, :, a * 128 : (a + 1) * 128] = hit_o
-            for b in range(2):
-                mask_c[k, b * 128 : (b + 1) * 128, a * 128 : (a + 1) * 128] = hit_c
+            mask_c[k, a * 128 : (a + 1) * 128, :] = hit_c
 
     for copy in tell:
         copy.wait_recv()
@@ -296,20 +299,10 @@
         wide = jnp.concatenate([rows * mask_o[k] for k in range(classes)], axis=1)
         return mm(wide, toep_t[...])
 
-    def group(g):
+    def intake(g):
         pltpu.make_async_copy(recv.at[g], recv.at[g], rsem.at[g]).wait()
         got = recv[g].reshape(slots, LANES)
 
-        def pass_on():
-            pltpu.make_async_remote_copy(
-                src_ref=outbox.at[g],
-                dst_ref=inbox.at[g],
-                send_sem=cssem.at[g],
-                recv_sem=crsem.at[g],
-                device_id=(r, nxt),
-                device_id_type=MESH,
-            ).start()
-
         @pl.when(o < orders - 1)
         def _():
             base_out[...] = route((mm(wo_hi[...], got) + mm(wo_lo[...], got)).astype(BF))
@@ -317,34 +310,58 @@
         @pl.when(o == 0)
         def _():
             outbox[g] = base_out[...].astype(BF)
-            pass_on()
-
-        lat[...] = mm(w_hi[...], got) + mm(w_lo[...], got)
-
+            pass_on(g)
+
+        lat[g] = mm(w_hi[...], got) + mm(w_lo[...], got)
+
+    def pass_on(g):
+        pltpu.make_async_remote_copy(
+            src_ref=outbox.at[g],
+            dst_ref=inbox.at[g],
+            send_sem=cssem.at[g],
+            recv_sem=crsem.at[g],
+            device_id=(r, nxt),
+            device_id_type=MESH,
+        ).start()
+
+    def level(g):
         @pl.when(o > 0)
         def _():
             pltpu.make_async_copy(inbox.at[g], inbox.at[g], crsem.at[g]).wait()
 
-            @pl.when(o < orders - 1)
-            def _():
-                moved = mm(perm[...], inbox[g]).astype(BF)
-                outbox[g] = (base_out[...] + route(moved)).astype(BF)
-                pass_on()
-
-            lat[...] = lat[...] + mm(scat[...], inbox[g])
+        @pl.when(jnp.logical_and(o > 0, o < orders - 1))
+        def _():
+            moved = mm(perm[...], inbox[g]).astype(BF)
+            outbox[g] = (base_out[...] + route(moved)).astype(BF)
+            pass_on(g)
+
+    def total(g):
+        @pl.when(o > 0)
+        def _():
+            lat[g] = lat[g] + mm(scat[...], inbox[g])
 
         def pair(h, c):
-            entering = lat[pl.ds(pl.multiple_of(h * 256, 256), 256), :].astype(BF)
-            wide = jnp.concatenate([entering * mask_c[k] for k in range(classes)], axis=1)
-            total = mm_nt(toep[...], wide)
+            entering = lat[g, pl.ds(pl.multiple_of(h * 256, 256), 256), :].astype(BF)
+            early, late_in = [
+                jnp.concatenate([entering[:, h : h + 128] * mask_c[k] for k in range(classes)], axis=1)
+                for h in (0, 128)
+            ]
+            flow = mm_nt(toep[:, 0 : classes * 128], early)
+            tail = mm_nt(toep[128:LANES, classes * 128 :], late_in)
             for m in range(2):
                 first = g * MG + h * 2 + m
-                out32[pl.ds(first, hours, stride=members), :] = total[
-                    0:hours, m * 128 : (m + 1) * 128
-                ]
+                cols = slice(m * 128, (m + 1) * 128)
+                out32[pl.ds(first, 128, stride=members), :] = flow[0:128, cols]
+                out32[pl.ds(first + 128 * members, hours - 128, stride=members), :] = (
+                    flow[128:hours, cols] + tail[0 : hours - 128, cols]
+                )
             return c
 
         lax.fori_loop(0, 2, pair, 0)
+
+    late = jnp.minimum(groups, (orders - 1 - o) * SPARE // (orders - 1))
+
+    lag = LAG + o // 3
 
     def turn(i, c):
         @pl.when(i < groups - AHEAD)
@@ -359,13 +376,24 @@
         def _():
             select(i - PICK)
 
-        @pl.when(i >= LAG)
-        def _():
-            group(i - LAG)
+        @pl.when(jnp.logical_and(i >= lag, i < groups + lag))
+        def _():
+            intake(i - lag)
+            level(i - lag)
+
+            @pl.when(i - lag < groups - late)
+            def _():
+                total(i - lag)
 
         return c
 
-    lax.fori_loop(0, groups + LAG, turn, 0)
+    lax.fori_loop(0, groups + LAG + 2, turn, 0)
+
+    def rest(g, c):
+        total(g)
+        return c
+
+    lax.fori_loop(groups - late, groups, rest, 0)
 
     for copy in tell:
         copy.wait_send()
@@ -435,7 +463,7 @@
             pltpu.VMEM((groups, NX, NZ, MG * 4, LANES), BF),
             pltpu.VMEM((groups, MG * panel, LANES), BF),
             pltpu.VMEM((groups, MG * panel, LANES), BF),
-            pltpu.VMEM((MG * reaches, LANES), F32),
+            pltpu.VMEM((groups, MG * reaches, LANES), F32),
             pltpu.VMEM((MG * panel, LANES), F32),
             pltpu.VMEM((5, 160, MG * rows), BF),
             pltpu.VMEM((MG * reaches, slots), BF),
@@ -445,7 +473,7 @@
             pltpu.VMEM((MG * panel, MG * panel), BF),
             pltpu.VMEM((MG * reaches, MG * panel), BF),
             pltpu.VMEM((classes, MG * panel, LANES), BF),
-            pltpu.VMEM((classes, 2 * reaches, LANES), BF),
+            pltpu.VMEM((classes, 2 * reaches, 128), BF),
             pltpu.VMEM((LANES, classes * LANES), BF),
             pltpu.VMEM((classes * LANES, LANES), BF),
             pltpu.SemaphoreType.DMA((4,)),

time: 72 us -> 69.5 us (0.965)
  Pallas kernels: 70.4 us -> 67.9 us
    pallas_call x1, Pallas kernels: 70.4 us -> 67.9 us  [local(): pl.pallas_call(functools.partial(kernel, sizes), out_shape=pltpu.VMEM((ho...]
where the time goes in v3:
time: 69.5 us; the launch traced here: 69.4 us
  Pallas kernels  67.9 us (98%)
  other arithmetic  1.46 us (2%)
    pallas_call x1, Pallas kernels, local(): pl.pallas_call(functools.partial(kernel, sizes), out_shape=pltpu.VMEM((ho...  67.9 us
    convert_element_type x1, other arithmetic, local(): return flat.reshape(hours, members, reaches).astype(BF)  1.46 us

profile of v3, /device:TPU:25, one launch (start us, length us, event | category | flops | bytes accessed | tf_op | source)
XLA Modules:
  0.0 69.4 jit_solution(1471772016117345529)
XLA Ops:
  0.0 67.9 %route_levels.1 = f32[7680,128]{1,0:T(8,128)S(1)} custom-call(f32[1024,240]{1,0:T(8,128)} %bitcast.11, s32[1,128]{1,0:T(1,128)} %bitcast.15, s32[4,128]{1,0:T(4,128)} %bitcast.13, f32[4,128]{1,0:T(4,128)} %bitcast.14, s32[1,128]{1,0:T(1,128)} %bitcast.16, f32[8,240]{1,0:T(8,128)} %refs_5_.1, f32[1,8]{1,0:T(1,128)} %bitcast.17, s32[1,32]{1,0:T(1,128)} %bitcast.18, ...), custom_call_target="tpu_custom_call" | custom-call | tf_op jit(solution)/shard_map/route_levels/pallas_call | solution.py:449
  67.9 1.5 %convert_element_type.6 = bf16[7680,128]{1,0:T(8,128)(2,1)} convert(f32[7680,128]{1,0:T(8,128)S(1)} %route_levels.1) | non-fusion elementwise | flops 983040 | bytes 5898240 | tf_op jit(solution)/shard_map/convert_element_type | solution.py:496

commit v4 on v3

--- a/solution.py
+++ b/solution.py
@@ -49,6 +49,7 @@
     held,
     out32,
     insem,
+    turn_buf,
     own,
     near1,
     near2,
@@ -113,13 +114,18 @@
     lax.fori_loop(3, NX * 5, greet, 0)
     pl.semaphore_signal(barrier, inc=1, device_id=(r, prv), device_id_type=MESH)
 
-    own[:, :, 128:LANES] = jnp.zeros((groups, MG * 32, LANES - 128), BF)
+    filler = jnp.zeros((groups, 2, LANES - hours, 128), BF)
+    near1[:, :, hours:LANES] = filler
+    near2[:, :, hours:LANES] = filler
+    turn_buf[...] = jnp.zeros_like(turn_buf)
     loads[0].wait()
 
     def cast(g, c):
         rows = MG * 32
         start = pl.multiple_of(g * rows, rows)
-        own[g, :, 0:hours] = x_ref[pl.ds(start, rows), :].astype(BF)
+        own[g, 0:128] = x_ref[pl.ds(start, rows), 0:128].astype(BF)
+        turn_buf[:, 0 : hours - 128] = x_ref[pl.ds(start, rows), 128:hours]
+        own[g, 128:LANES] = turn_buf[...].T.astype(BF)
         return c
 
     lax.fori_loop(0, groups, cast, 0)
@@ -130,8 +136,8 @@
     def step1(g):
         for way in range(2):
             pltpu.make_async_remote_copy(
-                src_ref=own.at[g],
-                dst_ref=near1.at[g, way],
+                src_ref=own.at[g, pl.ds(0, hours)],
+                dst_ref=near1.at[g, way, pl.ds(0, hours)],
                 send_sem=s1s.at[g, way],
                 recv_sem=s1r.at[g, way],
                 device_id=at(0, 1 - 2 * way),
@@ -140,10 +146,11 @@
 
     def step2(g):
         for way in range(2):
-            pltpu.make_async_copy(near1.at[g, way], near1.at[g, way], s1r.at[g, way]).wait()
+            got = near1.at[g, way, pl.ds(0, hours)]
+            pltpu.make_async_copy(got, got, s1r.at[g, way]).wait()
             pltpu.make_async_remote_copy(
-                src_ref=near1.at[g, way],
-                dst_ref=near2.at[g, way],
+                src_ref=got,
+                dst_ref=near2.at[g, way, pl.ds(0, hours)],
                 send_sem=s2s.at[g, way],
                 recv_sem=s2r.at[g, way],
                 device_id=at(0, 1 - 2 * way),
@@ -251,11 +258,16 @@
 
     def select(g):
         for way in range(2):
-            pltpu.make_async_copy(near2.at[g, way], near2.at[g, way], s2r.at[g, way]).wait()
+            got = near2.at[g, way, pl.ds(0, hours)]
+            pltpu.make_async_copy(got, got, s2r.at[g, way]).wait()
         held_blocks = (near2[g, 1], near1[g, 1], own[g], near1[g, 0], near2[g, 0])
         for e in (0, 4, 1, 2, 3):
             outer = e == 0 or e == 4
-            taken = mm(sel[e] if outer else sel[e, 0:64, :], held_blocks[e]).astype(BF)
+            pick = sel[e] if outer else sel[e, 0:64, :]
+            block = held_blocks[e]
+            taken = jnp.concatenate(
+                [mm(pick, block[0:128]), mm_nt(pick, block[128:LANES])], axis=1
+            ).astype(BF)
             send_n[g, :, e] = taken[0:64].reshape(NX, MG * 4, LANES)
             if outer:
                 way = 0 if e == 4 else 1
@@ -400,8 +412,9 @@
 
     def drain(g, c):
         for way in range(2):
-            pltpu.make_async_copy(own.at[g], own.at[g], s1s.at[g, way]).wait()
-            pltpu.make_async_copy(near1.at[g, way], near1.at[g, way], s2s.at[g, way]).wait()
+            mine, passed = own.at[g, pl.ds(0, hours)], near1.at[g, way, pl.ds(0, hours)]
+            pltpu.make_async_copy(mine, mine, s1s.at[g, way]).wait()
+            pltpu.make_async_copy(passed, passed, s2s.at[g, way]).wait()
         sent = send_n.at[g, pl.ds(0, NX - 1)]
         pltpu.make_async_copy(sent, sent, nsem.at[g]).wait()
         pltpu.make_async_copy(send_f.at[g], send_f.at[g], fsem.at[g]).wait()
@@ -454,9 +467,10 @@
         scratch_shapes=[pltpu.VMEM(a.shape, a.dtype) for a in given]
         + [
             pltpu.SemaphoreType.DMA((len(given),)),
-            pltpu.VMEM((groups, MG * rows, LANES), BF),
-            pltpu.VMEM((groups, 2, MG * rows, LANES), BF),
-            pltpu.VMEM((groups, 2, MG * rows, LANES), BF),
+            pltpu.VMEM((MG * rows, 128), F32),
+            pltpu.VMEM((groups, LANES, MG * rows), BF),
+            pltpu.VMEM((groups, 2, LANES, MG * rows), BF),
+            pltpu.VMEM((groups, 2, LANES, MG * rows), BF),
             pltpu.VMEM((5, 1, 128), jnp.int32),
             pltpu.VMEM((groups, NX, 5, MG * 4, LANES), BF),
             pltpu.VMEM((groups, 2, 6, MG * 4, LANES), BF),

time: 69.5 us -> 69 us (level)
  no operation moved by 1% of the time
where the time goes in v4:
time: 69 us; the launch traced here: 68.9 us
  Pallas kernels  67.4 us (98%)
  other arithmetic  1.46 us (2%)
    pallas_call x1, Pallas kernels, local(): pl.pallas_call(functools.partial(kernel, sizes), out_shape=pltpu.VMEM((ho...  67.4 us
    convert_element_type x1, other arithmetic, local(): return flat.reshape(hours, members, reaches).astype(BF)  1.46 us

profile of v4, /device:TPU:25, one launch (start us, length us, event | category | flops | bytes accessed | tf_op | source)
XLA Modules:
  0.0 68.9 jit_solution(59263541201767806)
XLA Ops:
  0.0 67.4 %route_levels.1 = f32[7680,128]{1,0:T(8,128)S(1)} custom-call(f32[1024,240]{1,0:T(8,128)} %bitcast.11, s32[1,128]{1,0:T(1,128)} %bitcast.15, s32[4,128]{1,0:T(4,128)} %bitcast.13, f32[4,128]{1,0:T(4,128)} %bitcast.14, s32[1,128]{1,0:T(1,128)} %bitcast.16, f32[8,240]{1,0:T(8,128)} %refs_5_.1, f32[1,8]{1,0:T(1,128)} %bitcast.17, s32[1,32]{1,0:T(1,128)} %bitcast.18, ...), custom_call_target="tpu_custom_call" | custom-call | tf_op jit(solution)/shard_map/route_levels/pallas_call | solution.py:462
  67.4 1.5 %convert_element_type.6 = bf16[7680,128]{1,0:T(8,128)(2,1)} convert(f32[7680,128]{1,0:T(8,128)S(1)} %route_levels.1) | non-fusion elementwise | flops 983040 | bytes 5898240 | tf_op jit(solution)/shard_map/convert_element_type | solution.py:510

commit v5 on v4

--- a/solution.py
+++ b/solution.py
@@ -86,12 +86,15 @@
 ):
     hours, members, regions, orders, reaches, classes, panel = sizes
     x_ref, send_rows_ref, idx_ref, w_ref, cls_ref, shape_ref, rate_ref, outlets_ref, inc_ref = held
-    loads = [
-        pltpu.make_async_copy(given[i], held[i], insem.at[i]) for i in range(len(held))
+    groups = members // MG
+    soon = AHEAD * MG * 32
+    parts = (pl.ds(0, soon), pl.ds(soon, groups * MG * 32 - soon))
+    loads = [pltpu.make_async_copy(given[0].at[parts[0]], x_ref.at[parts[0]], insem.at[0])] + [
+        pltpu.make_async_copy(given[i], held[i], insem.at[i]) for i in range(1, len(held))
     ]
-    for load in loads:
+    others = pltpu.make_async_copy(given[0].at[parts[1]], x_ref.at[parts[1]], insem.at[len(held)])
+    for load in loads[:2] + [others] + loads[2:]:
         load.start()
-    groups = members // MG
     slots = regions * MG * 4
     r = lax.axis_index("region")
     o = lax.axis_index("order")
@@ -128,7 +131,7 @@
         own[g, 128:LANES] = turn_buf[...].T.astype(BF)
         return c
 
-    lax.fori_loop(0, groups, cast, 0)
+    lax.fori_loop(0, AHEAD, cast, 0)
     loads[1].wait()
     meta[2] = send_rows_ref[...]
     pl.semaphore_wait(barrier, NX * 5)
@@ -173,6 +176,8 @@
         copy.start()
     for g in range(1, AHEAD):
         step1(g)
+    others.wait()
+    lax.fori_loop(AHEAD, groups, cast, 0)
     for load in loads[2:]:
         load.wait()
 
@@ -466,7 +471,7 @@
         out_specs=pl.BlockSpec(memory_space=pltpu.VMEM),
         scratch_shapes=[pltpu.VMEM(a.shape, a.dtype) for a in given]
         + [
-            pltpu.SemaphoreType.DMA((len(given),)),
+            pltpu.SemaphoreType.DMA((len(given) + 1,)),
             pltpu.VMEM((MG * rows, 128), F32),
             pltpu.VMEM((groups, LANES, MG * rows), BF),
             pltpu.VMEM((groups, 2, LANES, MG * rows), BF),

time: 69 us -> 69 us (level)
  no operation moved by 1% of the time
where the time goes in v5:
time: 69 us; the launch traced here: 68.9 us
  Pallas kernels  67.5 us (98%)
  other arithmetic  1.46 us (2%)
    pallas_call x1, Pallas kernels, local(): pl.pallas_call(functools.partial(kernel, sizes), out_shape=pltpu.VMEM((ho...  67.5 us
    convert_element_type x1, other arithmetic, local(): return flat.reshape(hours, members, reaches).astype(BF)  1.46 us

profile of v5, /device:TPU:25, one launch (start us, length us, event | category | flops | bytes accessed | tf_op | source)
XLA Modules:
  0.0 68.9 jit_solution(16282240348173460374)
XLA Ops:
  0.0 67.5 %route_levels.1 = f32[7680,128]{1,0:T(8,128)S(1)} custom-call(f32[1024,240]{1,0:T(8,128)} %bitcast.11, s32[1,128]{1,0:T(1,128)} %bitcast.15, s32[4,128]{1,0:T(4,128)} %bitcast.13, f32[4,128]{1,0:T(4,128)} %bitcast.14, s32[1,128]{1,0:T(1,128)} %bitcast.16, f32[8,240]{1,0:T(8,128)} %refs_5_.1, f32[1,8]{1,0:T(1,128)} %bitcast.17, s32[1,32]{1,0:T(1,128)} %bitcast.18, ...), custom_call_target="tpu_custom_call" | custom-call | tf_op jit(solution)/shard_map/route_levels/pallas_call | solution.py:467
  67.5 1.5 %convert_element_type.6 = bf16[7680,128]{1,0:T(8,128)(2,1)} convert(f32[7680,128]{1,0:T(8,128)S(1)} %route_levels.1) | non-fusion elementwise | flops 983040 | bytes 5898240 | tf_op jit(solution)/shard_map/convert_element_type | solution.py:515

commit v6 on v5

--- a/solution.py
+++ b/solution.py
@@ -363,8 +363,8 @@
                 jnp.concatenate([entering[:, h : h + 128] * mask_c[k] for k in range(classes)], axis=1)
                 for h in (0, 128)
             ]
-            flow = mm_nt(toep[:, 0 : classes * 128], early)
-            tail = mm_nt(toep[128:LANES, classes * 128 :], late_in)
+            flow = mm_nt(toep[0:hours, 0 : classes * 128], early)
+            tail = mm_nt(toep[128:hours, classes * 128 :], late_in)
             for m in range(2):
                 first = g * MG + h * 2 + m
                 cols = slice(m * 128, (m + 1) * 128)

time: 69 us -> 69 us (level)
  no operation moved by 1% of the time
where the time goes in v6:
time: 69 us; the launch traced here: 68.9 us
  Pallas kernels  67.4 us (98%)
  other arithmetic  1.46 us (2%)
    pallas_call x1, Pallas kernels, local(): pl.pallas_call(functools.partial(kernel, sizes), out_shape=pltpu.VMEM((ho...  67.4 us
    convert_element_type x1, other arithmetic, local(): return flat.reshape(hours, members, reaches).astype(BF)  1.46 us

profile of v6, /device:TPU:25, one launch (start us, length us, event | category | flops | bytes accessed | tf_op | source)
XLA Modules:
  0.0 68.9 jit_solution(8829984088672075811)
XLA Ops:
  0.0 67.4 %route_levels.1 = f32[7680,128]{1,0:T(8,128)S(1)} custom-call(f32[1024,240]{1,0:T(8,128)} %bitcast.11, s32[1,128]{1,0:T(1,128)} %bitcast.15, s32[4,128]{1,0:T(4,128)} %bitcast.13, f32[4,128]{1,0:T(4,128)} %bitcast.14, s32[1,128]{1,0:T(1,128)} %bitcast.16, f32[8,240]{1,0:T(8,128)} %refs_5_.1, f32[1,8]{1,0:T(1,128)} %bitcast.17, s32[1,32]{1,0:T(1,128)} %bitcast.18, ...), custom_call_target="tpu_custom_call" | custom-call | tf_op jit(solution)/shard_map/route_levels/pallas_call | solution.py:467
  67.4 1.5 %convert_element_type.6 = bf16[7680,128]{1,0:T(8,128)(2,1)} convert(f32[7680,128]{1,0:T(8,128)S(1)} %route_levels.1) | non-fusion elementwise | flops 983040 | bytes 5898240 | tf_op jit(solution)/shard_map/convert_element_type | solution.py:515
